TPU v7x, 32 devices: a whole 2x2x4 slice. The times are simulated.
32 devices in a mesh: row: 8 (over z, x), col: 4 (over y, core).
Axes of the slice: x: 2, y: 2, z: 4, core: 2. Of those that a mesh axis runs over, the one named last changes fastest.
Arguments:
- field: bfloat16 [1, 64, 512, 512], P(None, None, 'row', 'col'), may hold values from -6 to 6
- x_weight: float32 [2, 2, 12, 64, 64], replicated, may hold values from -2 to 2
- y_weight: float32 [2, 2, 12, 64, 64], replicated, may hold values from -2 to 2
- up_weight: bfloat16 [2, 256, 64], replicated, may hold values from -0.75 to 0.75
- up_bias: float32 [2, 256], replicated, may hold values from -3 to 3
- down_weight: bfloat16 [2, 64, 256], replicated, may hold values from -0.375 to 0.375
Outputs:
- result: bfloat16 [1, 64, 512, 512], P(None, None, 'row', 'col')
All inputs are finite; a program needn't handle non-finite values.
Results may differ from a plain program's by a relative error of at most 0.025.
Values may be sent and summed in bfloat16 or wider, within the bound.
A program may use at most 64 MiB of HBM per device.

v0:
```python
import functools
import math

import jax
import jax.numpy as jnp
from jax import lax
from jax.experimental import pallas as pl
from jax.experimental.pallas import tpu as pltpu
from jax.sharding import PartitionSpec as P

MODES = 12
LAYERS = 2
MESH = pl.DeviceIdType.MESH
VMEM = pltpu.VMEM


def tables(total, start, count):
    pos = start + jnp.arange(count, dtype=jnp.int32)
    kays = jnp.arange(MODES, dtype=jnp.int32)
    phase = kays[:, None] * pos[None, :] % total
    angle = phase.astype(jnp.float32) * (2.0 * math.pi / total)
    both = jnp.stack([jnp.cos(angle), -jnp.sin(angle)], axis=1)
    factor = (jnp.where(kays == 0, 1.0, 2.0) / total).astype(jnp.float32)[:, None, None]
    forward = both.astype(jnp.bfloat16).reshape(2 * MODES, count)
    inverse = (both * factor).astype(jnp.bfloat16).reshape(2 * MODES, count)
    return forward, inverse


def dot(a, b, contract=((1,), (0,))):
    return lax.dot_general(a, b, (contract, ((), ())), preferred_element_type=jnp.float32)


def whole_kernel(
    nr, nc, field_in, fx_ref, gx_ref, fy_ref, gy_ref, wx, wy, up_in, bias_in, down_in, out,
    field, up_ref, bias_ref, down_ref, state, x_part, y_part, x_got, y_got, x_all, y_all, x_w, y_w, x_mat, y_mat,
    big, base, x_rows, y_rows, flat,
    w_sem, xs_send, xs_recv, ys_send, ys_recv, xg_send, xg_recv, yg_send, yg_recv,
):
    row = lax.axis_index("row")
    col = lax.axis_index("col")
    channels, lines, cols = field.shape
    both = 2 * MODES
    wide = 2 * channels
    x_own, y_own = cols // nr, lines // nc
    group = math.gcd(lines, 4)

    def row_peer(d):
        return (lax.rem(row + d, nr), col)

    def col_peer(d):
        return (row, lax.rem(col + d, nc))

    loads = [
        pltpu.make_async_copy(src, dst, w_sem.at[i])
        for i, (src, dst) in enumerate((
            (field_in, field), (wy, y_w), (wx, x_w), (up_in, up_ref), (bias_in, bias_ref),
            (down_in, down_ref),
        ))
    ]
    for load in loads:
        load.start()

    barrier = pltpu.get_barrier_semaphore()
    for d in range(1, nr):
        pl.semaphore_signal(barrier, inc=1, device_id=row_peer(d), device_id_type=MESH)
    for d in range(1, nc):
        pl.semaphore_signal(barrier, inc=1, device_id=col_peer(d), device_id_type=MESH)

    def copy(src, dst, send, recv, peer):
        made = pltpu.make_async_remote_copy(
            src_ref=src, dst_ref=dst, send_sem=send, recv_sem=recv,
            device_id=peer, device_id_type=MESH,
        )
        made.start()
        return made

    def stacked(x):
        return pl.ds(pl.multiple_of(x * channels, channels), channels)

    def mix(own, first, got, n, mat, result):
        for k in range(MODES):
            total = first[own, k].astype(jnp.float32)
            for d in range(1, n):
                total = total + got[d, k].astype(jnp.float32)
            result[own, k] = dot(total.astype(jnp.bfloat16), mat[k]).astype(jnp.bfloat16)

    loads[0].wait()
    for c in range(channels):
        big[pl.ds(c, lines, stride=channels), :] = field[c].astype(jnp.float32)

    for layer in range(LAYERS):
        for c in range(channels):
            if layer == 0:
                plane = field[c]
            else:
                plane = big[pl.ds(c, lines, stride=channels), :].astype(jnp.bfloat16)
            x_rows[pl.ds(c, both, stride=channels), :] = dot(fx_ref[...], plane)
        for k in range(MODES):
            turned = x_rows[k * wide:(k + 1) * wide, :].T
            for i in range(nr):
                x_part[i, k] = turned[i * x_own:(i + 1) * x_own].astype(jnp.bfloat16)
        if layer == 0:
            pl.semaphore_wait(barrier, nr + nc - 2)
        x_scatter = [
            copy(x_part.at[row_peer(d)[0]], x_got.at[layer, d], xs_send.at[layer, d],
                 xs_recv.at[layer, d], row_peer(d))
            for d in range(1, nr)
        ]

        def forward_y(step, carry):
            at = step * group
            many = []
            for j in range(group):
                fresh = big[stacked(at + j), :].astype(jnp.bfloat16)
                if layer == 0:
                    state[at + j] = fresh
                many.append(fresh)
            parts = dot(fy_ref[...], jnp.concatenate(many, axis=0), ((1,), (1,)))
            for j in range(group):
                here = slice(j * channels, (j + 1) * channels)
                y_rows[pl.ds(at + j, MODES, stride=lines), :] = jnp.concatenate(
                    [parts[:MODES, here], parts[16:16 + MODES, here]], axis=1
                )
            return carry

        lax.fori_loop(0, lines // group, forward_y, 0, unroll=4)
        for k in range(MODES):
            for i in range(nc):
                at = k * lines + i * y_own
                y_part[i, k] = y_rows[at:at + y_own, :].astype(jnp.bfloat16)
        y_scatter = [
            copy(y_part.at[col_peer(d)[1]], y_got.at[layer, d], ys_send.at[layer, d],
                 ys_recv.at[layer, d], col_peer(d))
            for d in range(1, nc)
        ]

        if layer == 0:
            for load in loads[1:]:
                load.wait()
        for w, mat in ((y_w, y_mat), (x_w, x_mat)):
            for k in range(MODES):
                real = w[layer, 0, k]
                imag = w[layer, 1, k]
                top = jnp.concatenate([real, imag], axis=1)
                bottom = jnp.concatenate([-imag, real], axis=1)
                mat[k] = jnp.concatenate([top, bottom], axis=0).astype(jnp.bfloat16)

        for made in y_scatter:
            made.wait()
        mix(col, y_part, y_got.at[layer], nc, y_mat, y_all.at[layer])
        y_gather = [
            copy(y_all.at[layer, col], y_all.at[layer, col], yg_send.at[layer, d],
                 yg_recv.at[layer, d], col_peer(d))
            for d in range(1, nc)
        ]
        for made in x_scatter:
            made.wait()
        mix(row, x_part, x_got.at[layer], nr, x_mat, x_all.at[layer])
        x_gather = [
            copy(x_all.at[layer, row], x_all.at[layer, row], xg_send.at[layer, d],
                 xg_recv.at[layer, d], row_peer(d))
            for d in range(1, nr)
        ]

        for made in y_gather:
            made.wait()
        for k in range(MODES):
            for i in range(nc):
                at = k * lines + i * y_own
                y_rows[at:at + y_own, :] = y_all[layer, i, k].astype(jnp.float32)

        def inverse_y(step, carry):
            at = step * group
            many = [
                y_rows[pl.ds(at + j, MODES, stride=lines), :].T.astype(jnp.bfloat16)
                for j in range(group)
            ]
            even = jnp.concatenate([one[:channels] for one in many], axis=0)
            odd = jnp.concatenate([one[channels:] for one in many], axis=0)
            back = dot(even, gy_ref[:MODES, :]) + dot(odd, gy_ref[16:16 + MODES, :])
            for j in range(group):
                line = back[j * channels:(j + 1) * channels]
                base[stacked(at + j), :] = state[at + j].astype(jnp.float32) + line
            return carry

        lax.fori_loop(0, lines // group, inverse_y, 0, unroll=4)

        for made in x_gather:
            made.wait()
        for k in range(MODES):
            for i in range(nr):
                flat[k, i * x_own:(i + 1) * x_own, :] = x_all[layer, i, k].astype(jnp.float32)
        for k in range(MODES):
            turned = flat[k].T
            for part in range(2):
                x_rows[pl.ds(2 * k + part, channels, stride=both), :] = turned[
                    part * channels:(part + 1) * channels
                ]
        for o in range(channels):
            modes = x_rows[o * both:(o + 1) * both, :].astype(jnp.bfloat16)
            big[pl.ds(o, lines, stride=channels), :] = dot(gx_ref[...], modes)

        bias = jnp.broadcast_to(bias_ref[layer:layer + 1, :], (8, bias_ref.shape[1])).T[:, :1]

        def feed(step, carry):
            at = step * group
            done = []
            for j in range(group):
                gline = (base[stacked(at + j), :] + big[stacked(at + j), :]).astype(jnp.bfloat16)
                hidden = dot(up_ref[layer], gline) + bias
                hidden = 0.5 * hidden * (1.0 + lax.erf(hidden * math.sqrt(0.5)))
                fresh = gline.astype(jnp.float32) + dot(
                    down_ref[layer], hidden.astype(jnp.bfloat16)
                )
                done.append(fresh.astype(jnp.bfloat16))
            for j in range(group):
                big[stacked(at + j), :] = done[j].astype(jnp.float32)
                if layer < LAYERS - 1:
                    state[at + j] = done[j]
            return carry

        lax.fori_loop(0, lines // group, feed, 0)

    for c in range(channels):
        out[c] = big[pl.ds(c, lines, stride=channels), :].astype(jnp.bfloat16)


def padded(table):
    even, odd = table[0::2], table[1::2]
    gap = ((0, 16 - MODES), (0, 0))
    return jnp.concatenate([jnp.pad(even, gap), jnp.pad(odd, gap)], axis=0)


def on_device(field, x_weight, y_weight, up_weight, up_bias, down_weight):
    planes, channels, lines, cols = field.shape
    nr, nc = lax.axis_size("row"), lax.axis_size("col")
    fx, gx = tables(lines * nr, lax.axis_index("row") * lines, lines)
    fy, gy = tables(cols * nc, lax.axis_index("col") * cols, cols)
    half, full = jnp.bfloat16, jnp.float32
    wide = 2 * channels
    x_shape = (nr, MODES, cols // nr, wide)
    y_shape = (nc, MODES, lines // nc, wide)
    dma = pltpu.SemaphoreType.DMA
    inside = pl.BlockSpec(memory_space=VMEM)
    outside = pl.BlockSpec(memory_space=pltpu.HBM)
    call = pl.pallas_call(
        functools.partial(whole_kernel, nr, nc),
        out_shape=jax.ShapeDtypeStruct((channels, lines, cols), half),
        in_specs=[outside] + [inside] * 4 + [outside] * 5,
        out_specs=inside,
        scratch_shapes=[
            VMEM((channels, lines, cols), half),
            VMEM(up_weight.shape, half),
            VMEM(up_bias.shape, full),
            VMEM(down_weight.shape, half),
            VMEM((lines, channels, cols), half),
            VMEM(x_shape, half),
            VMEM(y_shape, half),
            VMEM((LAYERS,) + x_shape, half),
            VMEM((LAYERS,) + y_shape, half),
            VMEM((LAYERS,) + x_shape, half),
            VMEM((LAYERS,) + y_shape, half),
            VMEM(x_weight.shape, full),
            VMEM(y_weight.shape, full),
            VMEM((MODES, wide, wide), half),
            VMEM((MODES, wide, wide), half),
            VMEM((lines * channels, cols), full),
            VMEM((lines * channels, cols), full),
            VMEM((2 * MODES * channels, cols), full),
            VMEM((MODES * lines, wide), full),
            VMEM((MODES, cols, wide), full),
            dma((6,)),
        ] + [dma((LAYERS, n)) for n in (nr, nr, nc, nc, nr, nr, nc, nc)],
        compiler_params=pltpu.CompilerParams(
            collective_id=0, has_side_effects=True, vmem_limit_bytes=48 << 20
        ),
        name="operator",
    )
    return jnp.stack([
        call(field[z], fx, gx.T, padded(fy), padded(gy), x_weight, y_weight,
             up_weight, up_bias, down_weight)
        for z in range(planes)
    ])


def solution(mesh):
    in_specs = (P(None, None, "row", "col"), P(), P(), P(), P(), P())
    out_specs = P(None, None, "row", "col")
    return jax.shard_map(
        on_device, mesh=mesh, in_specs=in_specs, out_specs=out_specs, check_vma=False
    )
```

profile of v0, /device:TPU:0, one launch (start us, length us, event | category | flops | bytes accessed | tf_op | source)
XLA Modules:
  0.0 83.9 jit_solution(4709943595699334133)
XLA Ops:
  0.0 0.1 mul.120
  0.1 0.1 mul.121
  0.2 0.2 fusion.13
  0.4 0.1 multiply_convert_fusion.1
  0.6 0.2 fusion.14
  0.8 0.1 copy.11
  0.9 1.0 %copy.13.up_in = bf16[2,256,64]{2,1,0:T(8,128)(2,1)S(1)} copy(bf16[2,256,64]{1,2,0:T(8,128)(2,1)} %param.9) | data formatting | bytes 131072 | tf_op args[3]
  1.9 0.0 copy-start
  1.9 1.4 %copy-done = f32[2,2,12,64,64]{4,3,2,1,0:T(8,128)S(1)} copy-done((f32[2,2,12,64,64]{4,3,2,1,0:T(8,128)S(1)}, f32[2,2,12,64,64]{4,3,2,1,0:T(8,128)}, u32[]{:S(2)}) %copy-start) | copy-done | bytes 786456
  3.3 0.0 copy-start.1
  3.3 1.4 %copy-done.1 = f32[2,2,12,64,64]{4,3,2,1,0:T(8,128)S(1)} copy-done((f32[2,2,12,64,64]{4,3,2,1,0:T(8,128)S(1)}, f32[2,2,12,64,64]{4,3,2,1,0:T(8,128)}, u32[]{:S(2)}) %copy-start.1) | copy-done | bytes 786456
  4.7 0.0 copy-start.2
  4.7 1.2 %copy-done.2 = bf16[1,64,64,128]{3,2,1,0:T(8,128)(2,1)S(1)} copy-done((bf16[1,64,64,128]{3,2,1,0:T(8,128)(2,1)S(1)}, bf16[1,64,64,128]{3,2,1,0:T(8,128)(2,1)}, u32[]{:S(2)}) %copy-start.2) | copy-done | bytes 1048600
  5.9 0.0 copy-start.3
  5.9 0.8 copy-done.3
  6.8 0.0 copy-start.4
  6.8 0.7 copy-done.4
  7.5 75.5 %operator.1 = bf16[64,64,128]{2,1,0:T(8,128)(2,1)S(1)} custom-call(bf16[64,64,128]{2,1,0:T(8,128)(2,1)S(1)} %bitcast.7, bf16[24,64]{1,0:T(8,128)(2,1)S(1)} %convert_element_type.50.fx_ref, bf16[64,24]{1,0:T(8,128)(2,1)S(1)} %fusion.gx_ref, bf16[32,128]{1,0:T(8,128)(2,1)S(1)} %get-tuple-element.9.fy_ref, bf16[32,128]{1,0:T(8,128)(2,1)S(1)} %get-tuple-element.10.gy_ref, ...), custom_call_target="tpu_custom_call" | custom-call | tf_op jit(solution)/shard_map/operator/pallas_call | solution.py:280
  82.9 1.0 %copy.15 = bf16[1,64,64,128]{3,2,1,0:T(8,128)(2,1)} copy(bf16[1,64,64,128]{3,2,1,0:T(8,128)(2,1)S(1)} %bitcast.6) | data formatting | bytes 2097152
  (13 shorter events, 0.2 us)
Async XLA Ops:
  1.9 1.4 %copy-start = (f32[2,2,12,64,64]{4,3,2,1,0:T(8,128)S(1)}, f32[2,2,12,64,64]{4,3,2,1,0:T(8,128)}, u32[]{:S(2)}) copy-start(f32[2,2,12,64,64]{4,3,2,1,0:T(8,128)} %wx.1) | copy-start | bytes 2359300
  3.3 1.4 %copy-start.1 = (f32[2,2,12,64,64]{4,3,2,1,0:T(8,128)S(1)}, f32[2,2,12,64,64]{4,3,2,1,0:T(8,128)}, u32[]{:S(2)}) copy-start(f32[2,2,12,64,64]{4,3,2,1,0:T(8,128)} %wy.1) | copy-start | bytes 2359300
  4.7 1.2 %copy-start.2 = (bf16[1,64,64,128]{3,2,1,0:T(8,128)(2,1)S(1)}, bf16[1,64,64,128]{3,2,1,0:T(8,128)(2,1)}, u32[]{:S(2)}) copy-start(bf16[1,64,64,128]{3,2,1,0:T(8,128)(2,1)} %param.6) | copy-start | bytes 3145732
  5.9 0.8 %copy-start.3 = (bf16[2,64,256]{2,1,0:T(8,128)(2,1)S(1)}, bf16[2,64,256]{2,1,0:T(8,128)(2,1)}, u32[]{:S(2)}) copy-start(bf16[2,64,256]{2,1,0:T(8,128)(2,1)} %down_in.1) | copy-start | bytes 196612
  6.8 0.7 copy-start.4
where the time goes:
time: 84.2 us; the launch traced here: 83.9 us
  Pallas kernels  75.5 us (90%)
  local copies, waits for them, and re-layouts  7.84 us (9%)
    pallas_call x1, Pallas kernels, on_device(): call(field[z], fx, gx.T, padded(fy), padded(gy), x_weight, y_weight, up_w...  75.5 us
    unnamed x12, local copies, waits for them, and re-layouts  7.49 us

commit v1 on v0

--- a/solution.py
+++ b/solution.py
@@ -208,8 +208,8 @@
             for j in range(group):
                 gline = (base[stacked(at + j), :] + big[stacked(at + j), :]).astype(jnp.bfloat16)
                 hidden = dot(up_ref[layer], gline) + bias
-                hidden = 0.5 * hidden * (1.0 + lax.erf(hidden * math.sqrt(0.5)))
-                fresh = gline.astype(jnp.float32) + dot(
+                hidden = hidden * (1.0 + lax.erf(hidden * math.sqrt(0.5)))
+                fresh = gline.astype(jnp.float32) + 0.5 * dot(
                     down_ref[layer], hidden.astype(jnp.bfloat16)
                 )
                 done.append(fresh.astype(jnp.bfloat16))
@@ -272,7 +272,7 @@
             dma((6,)),
         ] + [dma((LAYERS, n)) for n in (nr, nr, nc, nc, nr, nr, nc, nc)],
         compiler_params=pltpu.CompilerParams(
-            collective_id=0, has_side_effects=True, vmem_limit_bytes=48 << 20
+            collective_id=0, has_side_effects=True, vmem_limit_bytes=65000 << 10
         ),
         name="operator",
     )

time: 84.2 us -> 86.7 us (1.030)
  Pallas kernels: 75.5 us -> 79.8 us
  local copies, waits for them, and re-layouts: 7.84 us -> 4.21 us
  other arithmetic: 0.53 us -> 2.33 us
    pallas_call x1, Pallas kernels: 75.5 us -> 79.8 us  [on_device(): call(field[z], fx, gx.T, padded(fy), padded(gy), x_weight, y_weight, up_w...]
    unnamed x12 -> x2, local copies, waits for them, and re-layouts: 7.49 us -> 3.86 us
where the time goes in v1:
time: 86.7 us; the launch traced here: 86.4 us
  Pallas kernels  79.8 us (92%)
  local copies, waits for them, and re-layouts  4.21 us (5%)
  other arithmetic  2.33 us (3%)
    pallas_call x1, Pallas kernels, on_device(): call(field[z], fx, gx.T, padded(fy), padded(gy), x_weight, y_weight, up_w...  79.8 us
    unnamed x2, local copies, waits for them, and re-layouts  3.86 us

profile of v1, /device:TPU:0, one launch (start us, length us, event | category | flops | bytes accessed | tf_op | source)
XLA Modules:
  0.0 86.4 jit_solution(3904057040146933965)
XLA Ops:
  0.0 0.1 mul.120
  0.1 0.1 mul.121
  0.2 0.2 fusion.13
  0.4 0.1 multiply_convert_fusion.1
  0.6 0.6 fusion.5
  1.2 0.2 fusion.14
  1.4 0.6 convert_element_type.50.fx_ref
  2.0 0.1 copy.11
  2.1 0.6 fusion.gx_ref
  2.7 1.6 %copy.13.up_in = bf16[2,256,64]{2,1,0:T(8,128)(2,1)} copy(bf16[2,256,64]{1,2,0:T(8,128)(2,1)} %param.9) | data formatting | bytes 131072 | tf_op args[3]
  4.3 79.8 %operator.1 = bf16[64,64,128]{2,1,0:T(8,128)(2,1)} custom-call(bf16[64,64,128]{2,1,0:T(8,128)(2,1)} %bitcast.7, bf16[24,64]{1,0:T(8,128)(2,1)} %convert_element_type.50.fx_ref, bf16[64,24]{1,0:T(8,128)(2,1)} %fusion.gx_ref, bf16[32,128]{1,0:T(8,128)(2,1)} %get-tuple-element.9.fy_ref, bf16[32,128]{1,0:T(8,128)(2,1)} %get-tuple-element.10.gy_ref, ...), custom_call_target="tpu_custom_call" | custom-call | tf_op jit(solution)/shard_map/operator/pallas_call | solution.py:280
  84.1 2.3 %copy.15 = bf16[1,64,64,128]{3,2,1,0:T(8,128)(2,1)} copy(bf16[1,64,64,128]{3,2,1,0:T(8,128)(2,1)} %bitcast.6) | data formatting | bytes 2097152
  (10 shorter events, 0.2 us)
